TPU v7x, 32 devices: a whole 2x2x4 slice. The times are simulated.
32 devices in a mesh: query: 8 (over z, y), store: 4 (over x, core).
Axes of the slice: x: 2, y: 2, z: 4, core: 2. Of those that a mesh axis runs over, the one named last changes fastest.
Arguments:
- in_rows: bfloat16 [8, 16384, 64], P('query', 'store'), may hold values from -6 to 6
- out_rows: bfloat16 [8, 16384, 128], P('query', 'store'), may hold values from -0.625 to 0.625
- row_doc: int32 [8, 16384], P('query', 'store'), may hold values from 0 to 31
- row_pos: int32 [8, 16384], P('query', 'store'), may hold values from 0 to 255
- doc_len: int32 [8, 128], P('query', 'store'), may hold values from 128 to 256
- eig_in: float32 [64], replicated, may hold values from 0.25 to 2
- eig_out: float32 [128], replicated, may hold values from 0.25 to 2
- basis_in: float32 [64, 64], replicated, may hold values from -0.75 to 0.75
- basis_out: float32 [128, 128], replicated, may hold values from -0.5 to 0.5
- train_feats: bfloat16 [8, 768, 8192], P('query', 'store'), may hold values from -0.0625 to 0.0625
Outputs:
- scores: bfloat16 [8, 128, 768], P('query', None, 'store')
Inputs may be any that keep to these rules, and one draw needn't show every extreme that they name: On each device the 4096 rows form 8 blocks of 512 rows in order; the rows of block j belong to documents of group j in the same store column, and row_doc names the document among that destination's 32.
All inputs are finite; a program needn't handle non-finite values.
Results may differ from a plain program's by a relative error of at most 0.0049.
Values may be sent and summed in bfloat16 or wider, within the bound.
A program may use at most 64 MiB of HBM per device.

v0:
```python
import math
import jax
import jax.numpy as jnp
from jax import lax
from jax.sharding import PartitionSpec as P

damping = 0.1
highest = lax.Precision.HIGHEST


def from_behind(x, axis, by):
    devices = lax.axis_size(axis)
    return lax.ppermute(x, axis, [(i, (i + by) % devices) for i in range(devices)])


def precondition(gradients, scaling, basis_in, basis_out):
    in_width = basis_in.shape[0]
    out_width = basis_out.shape[0]
    doc_count = gradients.shape[1] // in_width
    rotated = jnp.dot(basis_out.T, gradients, precision=highest)
    turned = jnp.dot(rotated.reshape(out_width * doc_count, in_width), basis_in, precision=highest)
    turned = turned.reshape(out_width, doc_count, in_width) * scaling[:, None, :]
    restored = jnp.dot(
        basis_out, turned.reshape(out_width, doc_count * in_width), precision=highest
    )
    final_map = jnp.dot(
        restored.reshape(out_width * doc_count, in_width), basis_in.T, precision=highest
    )
    final_map = final_map.reshape(out_width, doc_count, in_width)
    return (
        jnp.transpose(final_map, (1, 0, 2))
        .reshape(doc_count, out_width * in_width)
        .astype(jnp.bfloat16)
    )


def record(score_table, query_block, anchor, train_slab):
    partial_scores = lax.dot_general(
        query_block, train_slab, (((1,), (1,)), ((), ())), preferred_element_type=jnp.float32
    )
    return lax.dynamic_update_slice_in_dim(
        score_table, partial_scores.astype(jnp.bfloat16), anchor * query_block.shape[0], 0
    )


def on_device(
    in_rows, out_rows, row_doc, row_pos, doc_len, eig_in, eig_out, basis_in, basis_out, train_feats
):
    doc_count = doc_len.shape[1]
    in_width = in_rows.shape[2]
    packed_keys = row_doc * 65536 + row_pos
    inputs_side, grads_side, keys_side = (
        lax.all_to_all(in_rows, "query", split_axis=1, concat_axis=1, tiled=True),
        lax.all_to_all(out_rows, "query", split_axis=1, concat_axis=1, tiled=True),
        lax.all_to_all(packed_keys, "query", split_axis=1, concat_axis=1, tiled=True),
    )
    inputs_side = inputs_side[0]
    grads_side = grads_side[0]
    keys_side = keys_side[0]
    doc_of_row = keys_side // 65536
    pos_of_row = keys_side % 65536
    live_mask = (doc_of_row[:, None] == jnp.arange(doc_count, dtype=jnp.int32)[None, :]) & (
        pos_of_row[:, None] < doc_len[0][None, :]
    )
    weights = live_mask.astype(jnp.bfloat16)
    row_count = inputs_side.shape[0]
    row_span = math.gcd(row_count, 1024)

    def accumulate(turn_index, running):
        row_start = turn_index * row_span
        x_part = lax.dynamic_slice_in_dim(inputs_side, row_start, row_span, 0)
        g_part = lax.dynamic_slice_in_dim(grads_side, row_start, row_span, 0)
        w_part = lax.dynamic_slice_in_dim(weights, row_start, row_span, 0)
        spread = (w_part[:, :, None] * x_part[:, None, :]).reshape(row_span, doc_count * in_width)
        return running + lax.dot_general(
            g_part, spread, (((0,), (0,)), ((), ())), preferred_element_type=jnp.float32
        )

    gradients = jnp.zeros((grads_side.shape[1], doc_count * in_width), jnp.float32)
    gradients = lax.fori_loop(0, row_count // row_span, accumulate, gradients)
    scaling = 1.0 / (eig_out[:, None] * eig_in[None, :] + damping)
    query_block = precondition(gradients, scaling, basis_in, basis_out)
    train_slab = train_feats[0]
    store_count = lax.axis_size("store")
    own_index = lax.axis_index("store")
    score_table = jnp.zeros((store_count * doc_count, train_slab.shape[0]), jnp.bfloat16)

    def travel(carry, visit_index):
        moving, table_now = carry
        table_now = record(table_now, moving, (own_index - visit_index) % store_count, train_slab)
        moving = from_behind(moving, "store", 1)
        return ((moving, table_now), None)

    (moving, score_table), _ = lax.scan(
        travel, (query_block, score_table), jnp.arange(store_count - 1, dtype=jnp.int32)
    )
    score_table = record(
        score_table, moving, (own_index - (store_count - 1)) % store_count, train_slab
    )
    return score_table[None]


def solution(mesh):
    placed = (
        P("query", "store", None),
        P("query", "store", None),
        P("query", "store"),
        P("query", "store"),
        P("query", "store"),
        P(),
        P(),
        P(),
        P(),
        P("query", "store", None),
    )
    return jax.shard_map(
        on_device, mesh=mesh, in_specs=placed, out_specs=P("query", None, "store"), check_vma=False
    )
```

profile of v0, /device:TPU:0, one launch (start us, length us, event | category | flops | bytes accessed | tf_op | source)
XLA Modules:
  0.0 183.5 jit_solution(18066739965186172153)
XLA Ops:
  0.0 1.4 multiply_add_fusion
  1.4 7.3 %all-to-all-start.1 = ((s32[1,8,512]{2,0,1:T(1,128)}), s32[1,8,512]{2,0,1:T(1,128)S(1)}, u32[]{:S(2)}, u32[]{:S(2)}) async-start(s32[1,8,512]{2,0,1:T(1,128)} %bitcast.1), calls=%async_computation.1 | async-start | bytes 32768 | tf_op jit(solution)/shard_map/all_to_all | solution.py:55
  8.7 4.9 %copy.27 = bf16[1,4096,64]{2,0,1:T(2,128)(2,1)S(1)} copy(bf16[1,4096,64]{1,2,0:T(8,128)(2,1)} %param.14) | data formatting | bytes 1048576 | tf_op args[0]
  14.1 22.3 %reduce.1 = bf16[4096,64]{1,0:T(8,128)(2,1)S(1)} reduce(bf16[4096,1,64]{2,1,0:T(2,128)(2,1)S(1)} %bitcast.60, bf16[]{:T(256)} %broadcast.96), dimensions={1}, to_apply=%bitcast.31.reduce_sub_computation | reduce | bytes 1048578
  36.4 1.5 reshape.110
  37.9 6.0 %all-to-all-start.2 = ((bf16[8,2,16384]{2,1,0:T(2,128)(2,1)}), bf16[8,2,16384]{2,1,0:T(2,128)(2,1)}, u32[]{:S(2)}, u32[]{:S(2)}) async-start(bf16[8,2,16384]{2,1,0:T(2,128)(2,1)} %reshape.110), calls=%async_computation.2 | async-start | bytes 1048576 | tf_op jit(solution)/shard_map/all_to_all | solution.py:53
  43.9 3.2 %copy.39 = bf16[1,4096,128]{2,0,1:T(2,128)(2,1)S(1)} copy(bf16[1,4096,128]{2,1,0:T(8,128)(2,1)} %param.15) | data formatting | bytes 2097152 | tf_op args[1]
  47.1 22.3 %reduce = bf16[4096,128]{1,0:T(8,128)(2,1)S(1)} reduce(bf16[4096,1,128]{2,1,0:T(2,128)(2,1)S(1)} %bitcast.62, bf16[]{:T(256)} %broadcast.96), dimensions={1}, to_apply=%bitcast.45.reduce_sub_computation | reduce | bytes 2097154
  69.5 1.1 reshape.108
  70.6 6.0 %all-to-all-start = ((bf16[8,2,32768]{2,1,0:T(2,128)(2,1)}), bf16[8,2,32768]{2,1,0:T(2,128)(2,1)}, u32[]{:S(2)}, u32[]{:S(2)}) async-start(bf16[8,2,32768]{2,1,0:T(2,128)(2,1)} %reshape.108), calls=%async_computation | async-start | bytes 2097152 | tf_op jit(solution)/shard_map/all_to_all | solution.py:54
  76.9 4.1 %reshape.111 = bf16[4096,1,64]{2,1,0:T(2,128)(2,1)S(1)} reshape(bf16[8,2,16384]{2,1,0:T(2,128)(2,1)} %all-to-all-done.2) | data formatting | bytes 1048576
  81.0 3.6 %copy.28 = bf16[1,4096,64]{1,2,0:T(8,128)(2,1)} copy(bf16[1,4096,64]{2,0,1:T(2,128)(2,1)S(1)} %bitcast.59) | data formatting | bytes 1048576 | tf_op jit(solution)/shard_map/all_to_all | solution.py:53
  84.7 16.9 %all-to-all-done = bf16[8,2,32768]{2,1,0:T(2,128)(2,1)} async-done(((bf16[8,2,32768]{2,1,0:T(2,128)(2,1)}), bf16[8,2,32768]{2,1,0:T(2,128)(2,1)}, u32[]{:S(2)}, u32[]{:S(2)}) %all-to-all-start) | async-done | bytes 1048608 | tf_op jit(solution)/shard_map/all_to_all | solution.py:54
  101.5 4.3 %reshape.109 = bf16[4096,1,128]{2,1,0:T(2,128)(2,1)S(1)} reshape(bf16[8,2,32768]{2,1,0:T(2,128)(2,1)} %all-to-all-done) | data formatting | bytes 2097152
  105.9 1.1 copy.38
  107.0 28.7 %while.29 = (s32[]{:T(128)}, f32[128,2048]{1,0:T(8,128)S(1)}, bf16[4096,128]{1,0:T(8,128)(2,1)}, bf16[4096,32]{0,1:T(8,128)(2,1)S(1)}, bf16[4096,64]{0,1:T(8,128...) while((s32[]{:T(128)}, f32[128,2048]{1,0:T(8,128)S(1)}, bf16[4096,128]{1,0:T(8,128)(2,1)}, ...), condition=%wide.region_1.2_spmd.clone, body=%wide.region_0.1_spmd.clone.sunk | while | flops 539492352 | bytes 11337897 | solution.py:80
  107.0 0.9 constant_dynamic-slice_fusion.4
  107.9 2.2 %broadcast_multiply_fusion.2 = bf16[1024,32,64]{0,2,1:T(8,128)(2,1)} fusion(bf16[1024,64]{0,1:T(8,128)(2,1)S(1)} %constant_dynamic-slice_fusion.4, bf16[1024,32]{0,1:T(8,128)(2,1)S(1)} %constant_dynamic-slice_fusion.5), kind=kLoop, calls=%fused_computation.3.clone.1 | loop fusion | flops 2097152 | bytes 4390912 | tf_op jit(solution)/shard_map/while/body/eval_jaxpr/mul | solution.py:74
  110.1 4.0 %convolution_add_fusion.2 = f32[128,2048]{1,0:T(8,128)S(1)} fusion(bf16[1024,2048]{0,1:T(8,128)(2,1)} %bitcast.56, f32[128,2048]{1,0:T(8,128)S(1)} %get-tuple-element.306, pred[]{:T(512)S(6)} %compare.16, bf16[4096,128]{1,0:T(8,128)(2,1)} %get-tuple-element.316, s32[]{:T(128)S(6)} %select_n.65), kind=kOutput, calls=%fused_computation.2.clone.1 | convolution fusion | flops 537395200 | bytes 6553605 | tf_op jit(solution)/shard_map/while/body/eval_jaxpr/dot_general | solution.py:75
  114.1 0.9 constant_dynamic-slice_fusion.4
  115.1 2.2 %broadcast_multiply_fusion.2 = bf16[1024,32,64]{0,2,1:T(8,128)(2,1)} fusion(bf16[1024,64]{0,1:T(8,128)(2,1)S(1)} %constant_dynamic-slice_fusion.4, bf16[1024,32]{0,1:T(8,128)(2,1)S(1)} %constant_dynamic-slice_fusion.5), kind=kLoop, calls=%fused_computation.3.clone.1 | loop fusion | flops 2097152 | bytes 4390912 | tf_op jit(solution)/shard_map/while/body/eval_jaxpr/mul | solution.py:74
  117.3 4.0 %convolution_add_fusion.2 = f32[128,2048]{1,0:T(8,128)S(1)} fusion(bf16[1024,2048]{0,1:T(8,128)(2,1)} %bitcast.56, f32[128,2048]{1,0:T(8,128)S(1)} %get-tuple-element.306, pred[]{:T(512)S(6)} %compare.16, bf16[4096,128]{1,0:T(8,128)(2,1)} %get-tuple-element.316, s32[]{:T(128)S(6)} %select_n.65), kind=kOutput, calls=%fused_computation.2.clone.1 | convolution fusion | flops 537395200 | bytes 6553605 | tf_op jit(solution)/shard_map/while/body/eval_jaxpr/dot_general | solution.py:75
  121.3 0.9 constant_dynamic-slice_fusion.4
  122.3 2.2 %broadcast_multiply_fusion.2 = bf16[1024,32,64]{0,2,1:T(8,128)(2,1)} fusion(bf16[1024,64]{0,1:T(8,128)(2,1)S(1)} %constant_dynamic-slice_fusion.4, bf16[1024,32]{0,1:T(8,128)(2,1)S(1)} %constant_dynamic-slice_fusion.5), kind=kLoop, calls=%fused_computation.3.clone.1 | loop fusion | flops 2097152 | bytes 4390912 | tf_op jit(solution)/shard_map/while/body/eval_jaxpr/mul | solution.py:74
  124.5 4.0 %convolution_add_fusion.2 = f32[128,2048]{1,0:T(8,128)S(1)} fusion(bf16[1024,2048]{0,1:T(8,128)(2,1)} %bitcast.56, f32[128,2048]{1,0:T(8,128)S(1)} %get-tuple-element.306, pred[]{:T(512)S(6)} %compare.16, bf16[4096,128]{1,0:T(8,128)(2,1)} %get-tuple-element.316, s32[]{:T(128)S(6)} %select_n.65), kind=kOutput, calls=%fused_computation.2.clone.1 | convolution fusion | flops 537395200 | bytes 6553605 | tf_op jit(solution)/shard_map/while/body/eval_jaxpr/dot_general | solution.py:75
  128.5 0.9 constant_dynamic-slice_fusion.4
  129.4 2.2 %broadcast_multiply_fusion.2 = bf16[1024,32,64]{0,2,1:T(8,128)(2,1)} fusion(bf16[1024,64]{0,1:T(8,128)(2,1)S(1)} %constant_dynamic-slice_fusion.4, bf16[1024,32]{0,1:T(8,128)(2,1)S(1)} %constant_dynamic-slice_fusion.5), kind=kLoop, calls=%fused_computation.3.clone.1 | loop fusion | flops 2097152 | bytes 4390912 | tf_op jit(solution)/shard_map/while/body/eval_jaxpr/mul | solution.py:74
  131.7 4.0 %convolution_add_fusion.2 = f32[128,2048]{1,0:T(8,128)S(1)} fusion(bf16[1024,2048]{0,1:T(8,128)(2,1)} %bitcast.56, f32[128,2048]{1,0:T(8,128)S(1)} %get-tuple-element.306, pred[]{:T(512)S(6)} %compare.16, bf16[4096,128]{1,0:T(8,128)(2,1)} %get-tuple-element.316, s32[]{:T(128)S(6)} %select_n.65), kind=kOutput, calls=%fused_computation.2.clone.1 | convolution fusion | flops 537395200 | bytes 6553605 | tf_op jit(solution)/shard_map/while/body/eval_jaxpr/dot_general | solution.py:75
  135.7 1.8 fusion.12
  137.5 1.1 convolution_multiply_fusion
  138.6 1.0 fusion.13
  139.6 1.9 %fusion.3 = bf16[32,128,64]{1,2,0:T(8,128)(2,1)} fusion(f32[128,32,64]{0,2,1:T(8,128)S(1)} %bitcast.66, f32[64,64]{1,0:T(8,128)S(1)} %copy-done.2), kind=kOutput, calls=%fused_computation.10 | convolution fusion | flops 201588736 | bytes 1589248 | tf_op jit(solution)/shard_map/dot_general | solution.py:26
  141.5 2.4 %copy.30 = bf16[32,128,64]{2,1,0:T(8,128)(2,1)} copy(bf16[32,128,64]{1,2,0:T(8,128)(2,1)} %fusion.3) | data formatting | bytes 1048576 | tf_op jit(solution)/shard_map/convert_element_type | solution.py:33
  143.9 2.7 %convert_element_type.24 = bf16[32,8192]{1,0:T(8,128)(2,1)} reshape(bf16[32,128,64]{2,1,0:T(8,128)(2,1)} %copy.30) | data formatting | bytes 1048576 | tf_op jit(solution)/shard_map/convert_element_type | solution.py:33
  146.6 32.4 %while.28 = (s32[]{:T(128)}, bf16[32,8192]{1,0:T(8,128)(2,1)}, bf16[128,192]{1,0:T(8,128)(2,1)S(1)}, bf16[192,8192]{1,0:T(8,128)(2,1)S(1)}, s32[3]{0:T(128)S(1)}...) while((s32[]{:T(128)}, bf16[32,8192]{1,0:T(8,128)(2,1)}, ...), condition=%wide.region_3.4_spmd, body=%wide.region_2.3_spmd.sunk | while | flops 100669456 | bytes 6832468 | solution.py:94
  146.6 1.9 %copy.51 = bf16[32,8192]{1,0:T(8,128)(2,1)} copy(bf16[32,8192]{1,0:T(8,128)(2,1)} %get-tuple-element.336) | data formatting | bytes 1048576 | tf_op jit(solution)/shard_map
  148.5 0.6 dynamic_slice.39
  149.7 2.1 %fusion.31 = bf16[128,192]{1,0:T(8,128)(2,1)S(1)} fusion(bf16[128,192]{1,0:T(8,128)(2,1)S(1)} %get-tuple-element.337, s32[]{:T(128)S(6)} %select_n.64, bf16[32,8192]{1,0:T(8,128)(2,1)} %copy.51, bf16[192,8192]{1,0:T(8,128)(2,1)S(1)} %get-tuple-element.350), kind=kOutput, calls=%fused_computation.1.clone.1 | convolution fusion | flops 100669440 | bytes 3686404 | tf_op jit(solution)/shard_map/while/body/eval_jaxpr/dot_general | solution.py:38
  151.8 5.6 %collective-permute-done = bf16[32,8192]{1,0:T(8,128)(2,1)} collective-permute-done((bf16[32,8192]{1,0:T(8,128)(2,1)}, bf16[32,8192]{1,0:T(8,128)(2,1)}, u32[]{:S(2)}, u32[]{:S(2)}) %collective-permute-start) | collective-permute-done | bytes 524320 | tf_op jit(solution)/shard_map/while/body/eval_jaxpr/ppermute | solution.py:13
  157.4 1.9 %copy.51 = bf16[32,8192]{1,0:T(8,128)(2,1)} copy(bf16[32,8192]{1,0:T(8,128)(2,1)} %get-tuple-element.336) | data formatting | bytes 1048576 | tf_op jit(solution)/shard_map
  160.5 2.1 %fusion.31 = bf16[128,192]{1,0:T(8,128)(2,1)S(1)} fusion(bf16[128,192]{1,0:T(8,128)(2,1)S(1)} %get-tuple-element.337, s32[]{:T(128)S(6)} %select_n.64, bf16[32,8192]{1,0:T(8,128)(2,1)} %copy.51, bf16[192,8192]{1,0:T(8,128)(2,1)S(1)} %get-tuple-element.350), kind=kOutput, calls=%fused_computation.1.clone.1 | convolution fusion | flops 100669440 | bytes 3686404 | tf_op jit(solution)/shard_map/while/body/eval_jaxpr/dot_general | solution.py:38
  162.6 5.6 %collective-permute-done = bf16[32,8192]{1,0:T(8,128)(2,1)} collective-permute-done((bf16[32,8192]{1,0:T(8,128)(2,1)}, bf16[32,8192]{1,0:T(8,128)(2,1)}, u32[]{:S(2)}, u32[]{:S(2)}) %collective-permute-start) | collective-permute-done | bytes 524320 | tf_op jit(solution)/shard_map/while/body/eval_jaxpr/ppermute | solution.py:13
  168.2 1.9 %copy.51 = bf16[32,8192]{1,0:T(8,128)(2,1)} copy(bf16[32,8192]{1,0:T(8,128)(2,1)} %get-tuple-element.336) | data formatting | bytes 1048576 | tf_op jit(solution)/shard_map
  171.2 2.1 %fusion.31 = bf16[128,192]{1,0:T(8,128)(2,1)S(1)} fusion(bf16[128,192]{1,0:T(8,128)(2,1)S(1)} %get-tuple-element.337, s32[]{:T(128)S(6)} %select_n.64, bf16[32,8192]{1,0:T(8,128)(2,1)} %copy.51, bf16[192,8192]{1,0:T(8,128)(2,1)S(1)} %get-tuple-element.350), kind=kOutput, calls=%fused_computation.1.clone.1 | convolution fusion | flops 100669440 | bytes 3686404 | tf_op jit(solution)/shard_map/while/body/eval_jaxpr/dot_general | solution.py:38
  173.4 5.6 %collective-permute-done = bf16[32,8192]{1,0:T(8,128)(2,1)} collective-permute-done((bf16[32,8192]{1,0:T(8,128)(2,1)}, bf16[32,8192]{1,0:T(8,128)(2,1)}, u32[]{:S(2)}, u32[]{:S(2)}) %collective-permute-start) | collective-permute-done | bytes 524320 | tf_op jit(solution)/shard_map/while/body/eval_jaxpr/ppermute | solution.py:13
  179.0 0.7 copy.31
  179.7 2.1 %fusion.4 = bf16[1,32,192]{2,1,0:T(8,128)(2,1)S(1)} fusion(bf16[32,8192]{1,0:T(8,128)(2,1)} %get-tuple-element.180, bf16[1,192,8192]{2,1,0:T(8,128)(2,1)S(1)} %bitcast.58), kind=kOutput, calls=%fused_computation.12 | convolution fusion | flops 100669440 | bytes 3682304 | tf_op jit(solution)/shard_map/dot_general | solution.py:38
  181.9 1.6 dynamic_update_slice.10
  (31 shorter events, 2.2 us)
Async XLA Ops:
  0.0 135.7 %copy-start = (f32[128,128]{1,0:T(8,128)S(1)}, f32[128,128]{1,0:T(8,128)}, u32[]{:S(2)}) copy-start(f32[128,128]{1,0:T(8,128)} %param.22) | copy-start | bytes 196612
  1.4 36.5 %all-to-all-start.1 = ((s32[1,8,512]{2,0,1:T(1,128)}), s32[1,8,512]{2,0,1:T(1,128)S(1)}, u32[]{:S(2)}, u32[]{:S(2)}) async-start(s32[1,8,512]{2,0,1:T(1,128)} %bitcast.1), calls=%async_computation.1 | async-start | bytes 32768 | tf_op jit(solution)/shard_map/all_to_all | solution.py:55
  37.9 32.6 %all-to-all-start.2 = ((bf16[8,2,16384]{2,1,0:T(2,128)(2,1)}), bf16[8,2,16384]{2,1,0:T(2,128)(2,1)}, u32[]{:S(2)}, u32[]{:S(2)}) async-start(bf16[8,2,16384]{2,1,0:T(2,128)(2,1)} %reshape.110), calls=%async_computation.2 | async-start | bytes 1048576 | tf_op jit(solution)/shard_map/all_to_all | solution.py:53
  47.1 29.5 %copy-start.3 = (f32[64]{0:T(128)S(1)}, f32[64]{0:T(128)}, u32[]{:S(2)}) copy-start(f32[64]{0:T(128)} %param.19) | copy-start | bytes 772
  47.1 29.5 %copy-start.4 = (f32[128]{0:T(128)S(1)}, f32[128]{0:T(128)}, u32[]{:S(2)}) copy-start(f32[128]{0:T(128)} %param.20) | copy-start | bytes 1540
  47.1 29.6 %copy-start.5 = (s32[1,32]{1,0:T(1,128)S(1)}, s32[1,32]{1,0:T(1,128)}, u32[]{:S(2)}) copy-start(s32[1,32]{1,0:T(1,128)} %param.18) | copy-start | bytes 388
  70.6 31.0 %all-to-all-start = ((bf16[8,2,32768]{2,1,0:T(2,128)(2,1)}), bf16[8,2,32768]{2,1,0:T(2,128)(2,1)}, u32[]{:S(2)}, u32[]{:S(2)}) async-start(bf16[8,2,32768]{2,1,0:T(2,128)(2,1)} %reshape.108), calls=%async_computation | async-start | bytes 2097152 | tf_op jit(solution)/shard_map/all_to_all | solution.py:54
  107.0 30.5 %copy-start.2 = (f32[64,64]{1,0:T(8,128)S(1)}, f32[64,64]{1,0:T(8,128)}, u32[]{:S(2)}) copy-start(f32[64,64]{1,0:T(8,128)} %param.21) | copy-start | bytes 49156
  138.6 8.0 %copy-start.1 = (bf16[1,192,8192]{2,1,0:T(8,128)(2,1)S(1)}, bf16[1,192,8192]{2,1,0:T(8,128)(2,1)}, u32[]{:S(2)}) copy-start(bf16[1,192,8192]{2,1,0:T(8,128)(2,1)} %param.23) | copy-start | bytes 9437188
  148.5 8.9 %collective-permute-start = (bf16[32,8192]{1,0:T(8,128)(2,1)}, bf16[32,8192]{1,0:T(8,128)(2,1)}, u32[]{:S(2)}, u32[]{:S(2)}) collective-permute-start(bf16[32,8192]{1,0:T(8,128)(2,1)} %copy.51), channel_id=1, source_target_pairs={{0,1},{1,2},{2,3},{3,0},{4,5},{5,6},{6,7},{7,4},{8,9},{9,10},{10,1... | collective-permute-start | bytes 1572872 | tf_op jit(solution)/shard_map/while/body/eval_jaxpr/ppermute | solution.py:13
  159.3 8.9 %collective-permute-start = (bf16[32,8192]{1,0:T(8,128)(2,1)}, bf16[32,8192]{1,0:T(8,128)(2,1)}, u32[]{:S(2)}, u32[]{:S(2)}) collective-permute-start(bf16[32,8192]{1,0:T(8,128)(2,1)} %copy.51), channel_id=1, source_target_pairs={{0,1},{1,2},{2,3},{3,0},{4,5},{5,6},{6,7},{7,4},{8,9},{9,10},{10,1... | collective-permute-start | bytes 1572872 | tf_op jit(solution)/shard_map/while/body/eval_jaxpr/ppermute | solution.py:13
  170.1 8.9 %collective-permute-start = (bf16[32,8192]{1,0:T(8,128)(2,1)}, bf16[32,8192]{1,0:T(8,128)(2,1)}, u32[]{:S(2)}, u32[]{:S(2)}) collective-permute-start(bf16[32,8192]{1,0:T(8,128)(2,1)} %copy.51), channel_id=1, source_target_pairs={{0,1},{1,2},{2,3},{3,0},{4,5},{5,6},{6,7},{7,4},{8,9},{9,10},{10,1... | collective-permute-start | bytes 1572872 | tf_op jit(solution)/shard_map/while/body/eval_jaxpr/ppermute | solution.py:13
where the time goes:
time: 185 us; the launch traced here: 184 us
  other arithmetic  55.2 us (30%)
  local copies, waits for them, and re-layouts  43 us (23%)
  waiting for transfers between devices  33.7 us (18%)
  matrix products  30.1 us (16%)
  starting transfers between devices  19.3 us (10%)
  loops' own time  1.96 us (1%)
    unnamed x3, other arithmetic  44.6 us
    unnamed x20, local copies, waits for them, and re-layouts  20.8 us
    all_to_all x1, waiting for transfers between devices, on_device(): lax.all_to_all(out_rows, 'query', split_axis=1, concat_axis=1, tiled=True)  16.9 us
    ppermute x3, waiting for transfers between devices, from_behind(): lax.ppermute(x, axis, [(i, (i + by) % devices) for i in range(devices)])  16.9 us
    dot_general x4, matrix products, accumulate(): lax.dot_general(g_part, spread, (((0,), (0,)), ((), ())), preferred_eleme...  15.9 us
    mul x4, other arithmetic, accumulate(): w_part[:, :, None] * x_part[:, None, :]  8.93 us
    dot_general x4, matrix products, record(): lax.dot_general(query_block, train_slab, (((1,), (1,)), ((), ())), prefer...  8.42 us
    all_to_all x1, starting transfers between devices, on_device(): lax.all_to_all(packed_keys, 'query', split_axis=1, concat_axis=1, tiled=T...  7.31 us
  transfers between devices with their start and end apart: 6, of which 4 were waited for; matrix products, arithmetic and copies ran while one was open for 39% of the time, Pallas kernels for 0%

commit v1 on v0

--- a/solution.py
+++ b/solution.py
@@ -6,6 +6,17 @@
 
 damping = 0.1
 highest = lax.Precision.HIGHEST
+
+
+def _lay_series(block_in, at_axis, incoming_x):
+    vec_out, formed = (block_in.shape[:at_axis], block_in.shape[at_axis + 1 :])
+    return jnp.moveaxis(block_in.reshape(*vec_out, incoming_x, -1, *formed), at_axis, 0)
+
+
+def bind_the_node(x0, k_dim):
+    y2 = list(x0.shape[1:])
+    y2[k_dim] *= x0.shape[0]
+    return jnp.moveaxis(x0, 0, k_dim).reshape(y2)
 
 
 def from_behind(x, axis, by):
@@ -49,9 +60,24 @@
     doc_count = doc_len.shape[1]
     in_width = in_rows.shape[2]
     packed_keys = row_doc * 65536 + row_pos
+
+    def unite_modes_for(packet, dev_axis, mat, content=1):
+        now, current_value = (lax.axis_size(dev_axis), lax.axis_index(dev_axis))
+        local_part = _lay_series(packet, mat, now)
+        local_out = local_part
+        for w in range(1, now):
+            outcome_arr, state_now = ((current_value + w) % now, (current_value - w) % now)
+            r2 = lax.dynamic_index_in_dim(local_part, outcome_arr, 0)
+            made = []
+            for at in range(now):
+                made.append((at, (at + w) % now))
+            later = lax.ppermute(r2, dev_axis, made)
+            local_out = lax.dynamic_update_slice_in_dim(local_out, later, state_now, axis=0)
+        return bind_the_node(local_out, content)
+
     inputs_side, grads_side, keys_side = (
         lax.all_to_all(in_rows, "query", split_axis=1, concat_axis=1, tiled=True),
-        lax.all_to_all(out_rows, "query", split_axis=1, concat_axis=1, tiled=True),
+        unite_modes_for(out_rows, "query", mat=1),
         lax.all_to_all(packed_keys, "query", split_axis=1, concat_axis=1, tiled=True),
     )
     inputs_side = inputs_side[0]

time: 185 us -> 163 us (0.88)
  the two profiles are of different devices: /device:TPU:0 before, /device:TPU:12 now
where the time goes in v1:
time: 163 us; the launch traced here: 162 us
  waiting for transfers between devices  41.5 us (25%)
  other arithmetic  35.4 us (22%)
  local copies, waits for them, and re-layouts  30.7 us (19%)
  matrix products  29.7 us (18%)
  starting transfers between devices  21.6 us (13%)
  loops' own time  2.21 us (1%)
    ppermute x7, waiting for transfers between devices, unite_modes_for(): later = lax.ppermute(r2, dev_axis, made)  24.8 us
    unnamed x2, other arithmetic  23.5 us
    ppermute x3, waiting for transfers between devices, from_behind(): lax.ppermute(x, axis, [(i, (i + by) % devices) for i in range(devices)])  16.7 us
    dot_general x4, matrix products, accumulate(): lax.dot_general(g_part, spread, (((0,), (0,)), ((), ())), preferred_eleme...  15.6 us
    unnamed x13, local copies, waits for them, and re-layouts  10.8 us
    ppermute x7, starting transfers between devices, unite_modes_for(): later = lax.ppermute(r2, dev_axis, made)  10.3 us
    mul x4, other arithmetic, accumulate(): w_part[:, :, None] * x_part[:, None, :]  8.99 us
    dot_general x4, matrix products, record(): lax.dot_general(query_block, train_slab, (((1,), (1,)), ((), ())), prefer...  8.42 us
  transfers between devices with their start and end apart: 12, of which 8 were waited for; matrix products, arithmetic and copies ran while one was open for 25% of the time, Pallas kernels for 0%

profile of v1, /device:TPU:12, one launch (start us, length us, event | category | flops | bytes accessed | tf_op | source)
XLA Modules:
  0.0 161.5 jit_solution(9681224367754543072)
XLA Ops:
  0.0 1.3 copy.58
  1.3 1.6 collective-permute-start.1
  2.9 1.4 multiply_add_fusion
  4.2 5.3 %all-to-all-start = ((s32[1,8,512]{2,0,1:T(1,128)}), s32[1,8,512]{2,0,1:T(1,128)S(1)}, u32[]{:S(2)}, u32[]{:S(2)}) async-start(s32[1,8,512]{2,0,1:T(1,128)} %bitcast.3), calls=%async_computation | async-start | bytes 32768 | tf_op jit(solution)/shard_map/all_to_all | solution.py:81
  10.5 3.8 %copy.25 = bf16[1,4096,64]{2,0,1:T(2,128)(2,1)} copy(bf16[1,4096,64]{1,2,0:T(8,128)(2,1)S(1)} %copy-done.2) | data formatting | bytes 1048576 | tf_op args[0]
  14.9 23.5 %reduce = bf16[4096,64]{1,0:T(8,128)(2,1)S(1)} reduce(bf16[4096,1,64]{2,1,0:T(2,128)(2,1)} %bitcast.58, bf16[]{:T(256)} %broadcast.114), dimensions={1}, to_apply=%bitcast.29.reduce_sub_computation | reduce | bytes 1048578
  38.4 1.5 reshape.108
  39.9 6.0 %all-to-all-start.1 = ((bf16[8,2,16384]{2,1,0:T(2,128)(2,1)}), bf16[8,2,16384]{2,1,0:T(2,128)(2,1)S(1)}, u32[]{:S(2)}, u32[]{:S(2)}) async-start(bf16[8,2,16384]{2,1,0:T(2,128)(2,1)} %reshape.108), calls=%async_computation.1 | async-start | bytes 1048576 | tf_op jit(solution)/shard_map/all_to_all | solution.py:79
  46.1 1.5 collective-permute-start.2
  47.7 1.0 collective-permute-start.3
  48.6 0.8 fusion.6
  49.4 2.0 %collective-permute-start.4 = (bf16[1,1,512,128]{3,2,0,1:T(8,128)(2,1)S(1)}, bf16[1,1,512,128]{3,2,0,1:T(8,128)(2,1)S(1)}, u32[]{:S(2)}, u32[]{:S(2)}) collective-permute-start(bf16[1,1,512,128]{3,2,0,1:T(8,128)(2,1)S(1)} %get-tuple-element.229), channel_id=1, source_target_pairs={{0,16},{4,20},{8,24},{12,28},{16,0},{20,4},{24,8},{28,12},{1,17},{... | collective-permute-start | bytes 393224 | tf_op jit(solution)/shard_map/ppermute | solution.py:74
  51.4 1.5 collective-permute-start.5
  52.9 2.4 %collective-permute-start.6 = (bf16[1,1,512,128]{3,2,0,1:T(8,128)(2,1)S(1)}, bf16[1,1,512,128]{3,2,0,1:T(8,128)(2,1)S(1)}, u32[]{:S(2)}, u32[]{:S(2)}) collective-permute-start(bf16[1,1,512,128]{3,2,0,1:T(8,128)(2,1)S(1)} %get-tuple-element.227), channel_id=1, source_target_pairs={{0,24},{4,28},{8,0},{12,4},{16,8},{20,12},{24,16},{28,20},{1,25},{... | collective-permute-start | bytes 393224 | tf_op jit(solution)/shard_map/ppermute | solution.py:74
  55.3 15.8 %collective-permute-done.2 = bf16[1,1,512,128]{3,2,0,1:T(8,128)(2,1)S(1)} collective-permute-done((bf16[1,1,512,128]{3,2,0,1:T(8,128)(2,1)S(1)}, bf16[1,1,512,128]{3,2,0,1:T(8,128)(2,1)S(1)}, u32[]{:S(2)}, u32[]{:S(2)}) %collective-permute-start.2) | collective-permute-done | bytes 131104 | tf_op jit(solution)/shard_map/ppermute | solution.py:74
  71.5 2.4 %collective-permute-done.3 = bf16[1,1,512,128]{3,2,0,1:T(8,128)(2,1)S(1)} collective-permute-done((bf16[1,1,512,128]{3,2,0,1:T(8,128)(2,1)S(1)}, bf16[1,1,512,128]{3,2,0,1:T(8,128)(2,1)S(1)}, u32[]{:S(2)}, u32[]{:S(2)}) %collective-permute-start.3) | collective-permute-done | bytes 131104 | tf_op jit(solution)/shard_map/ppermute | solution.py:74
  73.9 2.0 %collective-permute-done.4 = bf16[1,1,512,128]{3,2,0,1:T(8,128)(2,1)S(1)} collective-permute-done((bf16[1,1,512,128]{3,2,0,1:T(8,128)(2,1)S(1)}, bf16[1,1,512,128]{3,2,0,1:T(8,128)(2,1)S(1)}, u32[]{:S(2)}, u32[]{:S(2)}) %collective-permute-start.4) | collective-permute-done | bytes 131104 | tf_op jit(solution)/shard_map/ppermute | solution.py:74
  76.0 1.8 %collective-permute-done.6 = bf16[1,1,512,128]{3,2,0,1:T(8,128)(2,1)S(1)} collective-permute-done((bf16[1,1,512,128]{3,2,0,1:T(8,128)(2,1)S(1)}, bf16[1,1,512,128]{3,2,0,1:T(8,128)(2,1)S(1)}, u32[]{:S(2)}, u32[]{:S(2)}) %collective-permute-start.6) | collective-permute-done | bytes 131104 | tf_op jit(solution)/shard_map/ppermute | solution.py:74
  77.8 2.8 %collective-permute-done.7 = bf16[1,1,512,128]{3,2,0,1:T(8,128)(2,1)S(1)} collective-permute-done((bf16[1,1,512,128]{3,2,0,1:T(8,128)(2,1)S(1)}, bf16[1,1,512,128]{3,2,0,1:T(8,128)(2,1)S(1)}, u32[]{:S(2)}, u32[]{:S(2)}) %collective-permute-start.7) | collective-permute-done | bytes 131104 | tf_op jit(solution)/shard_map/ppermute | solution.py:74
  80.7 3.6 %reshape.109 = bf16[4096,1,64]{2,1,0:T(2,128)(2,1)} reshape(bf16[8,2,16384]{2,1,0:T(2,128)(2,1)S(1)} %all-to-all-done.1) | data formatting | bytes 1048576
  84.3 4.6 %copy.26 = bf16[1,4096,64]{1,2,0:T(8,128)(2,1)S(1)} copy(bf16[1,4096,64]{2,0,1:T(2,128)(2,1)} %bitcast.57) | data formatting | bytes 1048576 | tf_op jit(solution)/shard_map/all_to_all | solution.py:79
  88.9 24.8 %while.29 = (s32[]{:T(128)}, f32[128,2048]{1,0:T(8,128)S(1)}, bf16[4096,128]{1,0:T(8,128)(2,1)S(1)}, bf16[4096,32]{0,1:T(8,128)(2,1)S(1)}, bf16[4096,64]{0,1:T(8...) while((s32[]{:T(128)}, f32[128,2048]{1,0:T(8,128)S(1)}, ...), condition=%wide.region_1.2_spmd.clone, body=%wide.region_0.1_spmd.clone.sunk | while | flops 539492352 | bytes 11337889 | solution.py:106
  88.9 2.2 %broadcast_multiply_fusion.2 = bf16[1024,32,64]{0,2,1:T(8,128)(2,1)} fusion(bf16[1024,64]{0,1:T(8,128)(2,1)S(1)} %constant_dynamic-slice_fusion.11, bf16[1024,32]{0,1:T(8,128)(2,1)S(1)} %constant_dynamic-slice_fusion.12), kind=kLoop, calls=%fused_computation.3.clone.1 | loop fusion | flops 2097152 | bytes 4390912 | tf_op jit(solution)/shard_map/while/body/eval_jaxpr/mul | solution.py:100
  91.2 3.9 %convolution_add_fusion.2 = f32[128,2048]{1,0:T(8,128)S(1)} fusion(bf16[1024,2048]{0,1:T(8,128)(2,1)} %bitcast.51, f32[128,2048]{1,0:T(8,128)S(1)} %get-tuple-element.313, pred[]{:T(512)S(6)} %compare.30, bf16[4096,128]{1,0:T(8,128)(2,1)S(1)} %get-tuple-element.323, s32[]{:T(128)S(6)} %select_n.192), kind=kOutput, calls=%fused_computation.2.clone.1 | convolution fusion | flops 537395200 | bytes 6553605 | tf_op jit(solution)/shard_map/while/body/eval_jaxpr/dot_general | solution.py:101
  95.2 2.2 %broadcast_multiply_fusion.2 = bf16[1024,32,64]{0,2,1:T(8,128)(2,1)} fusion(bf16[1024,64]{0,1:T(8,128)(2,1)S(1)} %constant_dynamic-slice_fusion.11, bf16[1024,32]{0,1:T(8,128)(2,1)S(1)} %constant_dynamic-slice_fusion.12), kind=kLoop, calls=%fused_computation.3.clone.1 | loop fusion | flops 2097152 | bytes 4390912 | tf_op jit(solution)/shard_map/while/body/eval_jaxpr/mul | solution.py:100
  97.4 3.9 %convolution_add_fusion.2 = f32[128,2048]{1,0:T(8,128)S(1)} fusion(bf16[1024,2048]{0,1:T(8,128)(2,1)} %bitcast.51, f32[128,2048]{1,0:T(8,128)S(1)} %get-tuple-element.313, pred[]{:T(512)S(6)} %compare.30, bf16[4096,128]{1,0:T(8,128)(2,1)S(1)} %get-tuple-element.323, s32[]{:T(128)S(6)} %select_n.192), kind=kOutput, calls=%fused_computation.2.clone.1 | convolution fusion | flops 537395200 | bytes 6553605 | tf_op jit(solution)/shard_map/while/body/eval_jaxpr/dot_general | solution.py:101
  101.4 2.2 %broadcast_multiply_fusion.2 = bf16[1024,32,64]{0,2,1:T(8,128)(2,1)} fusion(bf16[1024,64]{0,1:T(8,128)(2,1)S(1)} %constant_dynamic-slice_fusion.11, bf16[1024,32]{0,1:T(8,128)(2,1)S(1)} %constant_dynamic-slice_fusion.12), kind=kLoop, calls=%fused_computation.3.clone.1 | loop fusion | flops 2097152 | bytes 4390912 | tf_op jit(solution)/shard_map/while/body/eval_jaxpr/mul | solution.py:100
  103.6 3.9 %convolution_add_fusion.2 = f32[128,2048]{1,0:T(8,128)S(1)} fusion(bf16[1024,2048]{0,1:T(8,128)(2,1)} %bitcast.51, f32[128,2048]{1,0:T(8,128)S(1)} %get-tuple-element.313, pred[]{:T(512)S(6)} %compare.30, bf16[4096,128]{1,0:T(8,128)(2,1)S(1)} %get-tuple-element.323, s32[]{:T(128)S(6)} %select_n.192), kind=kOutput, calls=%fused_computation.2.clone.1 | convolution fusion | flops 537395200 | bytes 6553605 | tf_op jit(solution)/shard_map/while/body/eval_jaxpr/dot_general | solution.py:101
  107.6 2.2 %broadcast_multiply_fusion.2 = bf16[1024,32,64]{0,2,1:T(8,128)(2,1)} fusion(bf16[1024,64]{0,1:T(8,128)(2,1)S(1)} %constant_dynamic-slice_fusion.11, bf16[1024,32]{0,1:T(8,128)(2,1)S(1)} %constant_dynamic-slice_fusion.12), kind=kLoop, calls=%fused_computation.3.clone.1 | loop fusion | flops 2097152 | bytes 4390912 | tf_op jit(solution)/shard_map/while/body/eval_jaxpr/mul | solution.py:100
  109.8 3.9 %convolution_add_fusion.2 = f32[128,2048]{1,0:T(8,128)S(1)} fusion(bf16[1024,2048]{0,1:T(8,128)(2,1)} %bitcast.51, f32[128,2048]{1,0:T(8,128)S(1)} %get-tuple-element.313, pred[]{:T(512)S(6)} %compare.30, bf16[4096,128]{1,0:T(8,128)(2,1)S(1)} %get-tuple-element.323, s32[]{:T(128)S(6)} %select_n.192), kind=kOutput, calls=%fused_computation.2.clone.1 | convolution fusion | flops 537395200 | bytes 6553605 | tf_op jit(solution)/shard_map/while/body/eval_jaxpr/dot_general | solution.py:101
  113.7 1.8 %fusion.12 = f32[2048,128]{1,0:T(8,128)S(1)} fusion(f32[128,2048]{1,0:T(8,128)S(1)} %get-tuple-element.178, f32[128,128]{1,0:T(8,128)S(1)} %copy-done), kind=kOutput, calls=%fused_computation.43 | convolution fusion | flops 402653184 | bytes 2162688 | tf_op jit(solution)/shard_map/dot_general | solution.py:31
  115.5 1.0 convolution_multiply_fusion
  116.6 1.0 fusion.13
  117.6 1.9 %fusion.3 = bf16[32,128,64]{1,2,0:T(8,128)(2,1)} fusion(f32[128,32,64]{0,2,1:T(8,128)S(1)} %bitcast.61, f32[64,64]{1,0:T(8,128)S(1)} %copy-done.3), kind=kOutput, calls=%fused_computation.10 | convolution fusion | flops 201588736 | bytes 1589248 | tf_op jit(solution)/shard_map/dot_general | solution.py:37
  119.5 2.4 %copy.28 = bf16[32,128,64]{2,1,0:T(8,128)(2,1)} copy(bf16[32,128,64]{1,2,0:T(8,128)(2,1)} %fusion.3) | data formatting | bytes 1048576 | tf_op jit(solution)/shard_map/convert_element_type | solution.py:44
  121.9 2.7 %convert_element_type.24 = bf16[32,8192]{1,0:T(8,128)(2,1)} reshape(bf16[32,128,64]{2,1,0:T(8,128)(2,1)} %copy.28) | data formatting | bytes 1048576 | tf_op jit(solution)/shard_map/convert_element_type | solution.py:44
  124.6 32.4 %while.28 = (s32[]{:T(128)}, bf16[32,8192]{1,0:T(8,128)(2,1)}, bf16[128,192]{1,0:T(8,128)(2,1)S(1)}, bf16[192,8192]{1,0:T(8,128)(2,1)S(1)}, s32[3]{0:T(128)S(1)}...) while((s32[]{:T(128)}, bf16[32,8192]{1,0:T(8,128)(2,1)}, ...), condition=%wide.region_3.4_spmd, body=%wide.region_2.3_spmd.sunk | while | flops 100669456 | bytes 6832468 | solution.py:120
  124.6 1.9 %copy.51 = bf16[32,8192]{1,0:T(8,128)(2,1)} copy(bf16[32,8192]{1,0:T(8,128)(2,1)} %get-tuple-element.343) | data formatting | bytes 1048576 | tf_op jit(solution)/shard_map
  127.7 2.1 %fusion.31 = bf16[128,192]{1,0:T(8,128)(2,1)S(1)} fusion(bf16[128,192]{1,0:T(8,128)(2,1)S(1)} %get-tuple-element.344, s32[]{:T(128)S(6)} %select_n.191, bf16[32,8192]{1,0:T(8,128)(2,1)} %copy.51, bf16[192,8192]{1,0:T(8,128)(2,1)S(1)} %get-tuple-element.357), kind=kOutput, calls=%fused_computation.1.clone.1 | convolution fusion | flops 100669440 | bytes 3686404 | tf_op jit(solution)/shard_map/while/body/eval_jaxpr/dot_general | solution.py:49
  129.9 5.6 %collective-permute-done = bf16[32,8192]{1,0:T(8,128)(2,1)} collective-permute-done((bf16[32,8192]{1,0:T(8,128)(2,1)}, bf16[32,8192]{1,0:T(8,128)(2,1)}, u32[]{:S(2)}, u32[]{:S(2)}) %collective-permute-start) | collective-permute-done | bytes 524320 | tf_op jit(solution)/shard_map/while/body/eval_jaxpr/ppermute | solution.py:24
  135.4 1.9 %copy.51 = bf16[32,8192]{1,0:T(8,128)(2,1)} copy(bf16[32,8192]{1,0:T(8,128)(2,1)} %get-tuple-element.343) | data formatting | bytes 1048576 | tf_op jit(solution)/shard_map
  138.5 2.1 %fusion.31 = bf16[128,192]{1,0:T(8,128)(2,1)S(1)} fusion(bf16[128,192]{1,0:T(8,128)(2,1)S(1)} %get-tuple-element.344, s32[]{:T(128)S(6)} %select_n.191, bf16[32,8192]{1,0:T(8,128)(2,1)} %copy.51, bf16[192,8192]{1,0:T(8,128)(2,1)S(1)} %get-tuple-element.357), kind=kOutput, calls=%fused_computation.1.clone.1 | convolution fusion | flops 100669440 | bytes 3686404 | tf_op jit(solution)/shard_map/while/body/eval_jaxpr/dot_general | solution.py:49
  140.6 5.6 %collective-permute-done = bf16[32,8192]{1,0:T(8,128)(2,1)} collective-permute-done((bf16[32,8192]{1,0:T(8,128)(2,1)}, bf16[32,8192]{1,0:T(8,128)(2,1)}, u32[]{:S(2)}, u32[]{:S(2)}) %collective-permute-start) | collective-permute-done | bytes 524320 | tf_op jit(solution)/shard_map/while/body/eval_jaxpr/ppermute | solution.py:24
  146.2 1.9 %copy.51 = bf16[32,8192]{1,0:T(8,128)(2,1)} copy(bf16[32,8192]{1,0:T(8,128)(2,1)} %get-tuple-element.343) | data formatting | bytes 1048576 | tf_op jit(solution)/shard_map
  149.3 2.1 %fusion.31 = bf16[128,192]{1,0:T(8,128)(2,1)S(1)} fusion(bf16[128,192]{1,0:T(8,128)(2,1)S(1)} %get-tuple-element.344, s32[]{:T(128)S(6)} %select_n.191, bf16[32,8192]{1,0:T(8,128)(2,1)} %copy.51, bf16[192,8192]{1,0:T(8,128)(2,1)S(1)} %get-tuple-element.357), kind=kOutput, calls=%fused_computation.1.clone.1 | convolution fusion | flops 100669440 | bytes 3686404 | tf_op jit(solution)/shard_map/while/body/eval_jaxpr/dot_general | solution.py:49
  151.4 5.6 %collective-permute-done = bf16[32,8192]{1,0:T(8,128)(2,1)} collective-permute-done((bf16[32,8192]{1,0:T(8,128)(2,1)}, bf16[32,8192]{1,0:T(8,128)(2,1)}, u32[]{:S(2)}, u32[]{:S(2)}) %collective-permute-start) | collective-permute-done | bytes 524320 | tf_op jit(solution)/shard_map/while/body/eval_jaxpr/ppermute | solution.py:24
  157.0 2.1 %fusion.4 = bf16[1,32,192]{2,1,0:T(8,128)(2,1)S(1)} fusion(bf16[32,8192]{1,0:T(8,128)(2,1)} %get-tuple-element.180, bf16[1,192,8192]{2,1,0:T(8,128)(2,1)S(1)} %bitcast.53), kind=kOutput, calls=%fused_computation.12 | convolution fusion | flops 100669440 | bytes 3682304 | tf_op jit(solution)/shard_map/dot_general | solution.py:49
  160.0 1.6 dynamic_update_slice.38
  (43 shorter events, 4.9 us)
Async XLA Ops:
  0.0 113.7 %copy-start = (f32[128,128]{1,0:T(8,128)S(1)}, f32[128,128]{1,0:T(8,128)}, u32[]{:S(2)}) copy-start(f32[128,128]{1,0:T(8,128)} %param.22) | copy-start | bytes 196612
  0.0 10.5 %copy-start.2 = (bf16[1,4096,64]{1,2,0:T(8,128)(2,1)S(1)}, bf16[1,4096,64]{1,2,0:T(8,128)(2,1)}, u32[]{:S(2)}) copy-start(bf16[1,4096,64]{1,2,0:T(8,128)(2,1)} %param.14) | copy-start | bytes 1572868
  1.3 44.6 %collective-permute-start.1 = (bf16[1,1,512,128]{3,2,0,1:T(8,128)(2,1)S(1)}, bf16[1,1,512,128]{3,2,0,1:T(8,128)(2,1)S(1)}, u32[]{:S(2)}, u32[]{:S(2)}) collective-permute-start(bf16[1,1,512,128]{3,2,0,1:T(8,128)(2,1)S(1)} %constant_dynamic-slice_fusion.8), channel_id=1, source_target_pairs={{0,4},{4,8},{8,12},{12,16},{16,20},{20,24},{24,28},{28,0},{1,5},{5... | collective-permute-start | bytes 393224 | tf_op jit(solution)/shard_map/ppermute | solution.py:74
  4.2 35.7 %all-to-all-start = ((s32[1,8,512]{2,0,1:T(1,128)}), s32[1,8,512]{2,0,1:T(1,128)S(1)}, u32[]{:S(2)}, u32[]{:S(2)}) async-start(s32[1,8,512]{2,0,1:T(1,128)} %bitcast.3), calls=%async_computation | async-start | bytes 32768 | tf_op jit(solution)/shard_map/all_to_all | solution.py:81
  39.9 40.7 %all-to-all-start.1 = ((bf16[8,2,16384]{2,1,0:T(2,128)(2,1)}), bf16[8,2,16384]{2,1,0:T(2,128)(2,1)S(1)}, u32[]{:S(2)}, u32[]{:S(2)}) async-start(bf16[8,2,16384]{2,1,0:T(2,128)(2,1)} %reshape.108), calls=%async_computation.1 | async-start | bytes 1048576 | tf_op jit(solution)/shard_map/all_to_all | solution.py:79
  46.1 24.9 %collective-permute-start.2 = (bf16[1,1,512,128]{3,2,0,1:T(8,128)(2,1)S(1)}, bf16[1,1,512,128]{3,2,0,1:T(8,128)(2,1)S(1)}, u32[]{:S(2)}, u32[]{:S(2)}) collective-permute-start(bf16[1,1,512,128]{3,2,0,1:T(8,128)(2,1)S(1)} %get-tuple-element.231), channel_id=1, source_target_pairs={{0,8},{4,12},{8,16},{12,20},{16,24},{20,28},{24,0},{28,4},{1,9},{5... | collective-permute-start | bytes 393224 | tf_op jit(solution)/shard_map/ppermute | solution.py:74
  47.7 26.2 %collective-permute-start.3 = (bf16[1,1,512,128]{3,2,0,1:T(8,128)(2,1)S(1)}, bf16[1,1,512,128]{3,2,0,1:T(8,128)(2,1)S(1)}, u32[]{:S(2)}, u32[]{:S(2)}) collective-permute-start(bf16[1,1,512,128]{3,2,0,1:T(8,128)(2,1)S(1)} %get-tuple-element.230), channel_id=1, source_target_pairs={{0,12},{4,16},{8,20},{12,24},{16,28},{20,0},{24,4},{28,8},{1,13},{... | collective-permute-start | bytes 393224 | tf_op jit(solution)/shard_map/ppermute | solution.py:74
  49.4 26.5 %collective-permute-start.4 = (bf16[1,1,512,128]{3,2,0,1:T(8,128)(2,1)S(1)}, bf16[1,1,512,128]{3,2,0,1:T(8,128)(2,1)S(1)}, u32[]{:S(2)}, u32[]{:S(2)}) collective-permute-start(bf16[1,1,512,128]{3,2,0,1:T(8,128)(2,1)S(1)} %get-tuple-element.229), channel_id=1, source_target_pairs={{0,16},{4,20},{8,24},{12,28},{16,0},{20,4},{24,8},{28,12},{1,17},{... | collective-permute-start | bytes 393224 | tf_op jit(solution)/shard_map/ppermute | solution.py:74
  51.4 24.5 %collective-permute-start.5 = (bf16[1,1,512,128]{3,2,0,1:T(8,128)(2,1)S(1)}, bf16[1,1,512,128]{3,2,0,1:T(8,128)(2,1)S(1)}, u32[]{:S(2)}, u32[]{:S(2)}) collective-permute-start(bf16[1,1,512,128]{3,2,0,1:T(8,128)(2,1)S(1)} %get-tuple-element.228), channel_id=1, source_target_pairs={{0,20},{4,24},{8,28},{12,0},{16,4},{20,8},{24,12},{28,16},{1,21},{... | collective-permute-start | bytes 393224 | tf_op jit(solution)/shard_map/ppermute | solution.py:74
  52.9 24.9 %collective-permute-start.6 = (bf16[1,1,512,128]{3,2,0,1:T(8,128)(2,1)S(1)}, bf16[1,1,512,128]{3,2,0,1:T(8,128)(2,1)S(1)}, u32[]{:S(2)}, u32[]{:S(2)}) collective-permute-start(bf16[1,1,512,128]{3,2,0,1:T(8,128)(2,1)S(1)} %get-tuple-element.227), channel_id=1, source_target_pairs={{0,24},{4,28},{8,0},{12,4},{16,8},{20,12},{24,16},{28,20},{1,25},{... | collective-permute-start | bytes 393224 | tf_op jit(solution)/shard_map/ppermute | solution.py:74
  71.1 9.6 %collective-permute-start.7 = (bf16[1,1,512,128]{3,2,0,1:T(8,128)(2,1)S(1)}, bf16[1,1,512,128]{3,2,0,1:T(8,128)(2,1)S(1)}, u32[]{:S(2)}, u32[]{:S(2)}) collective-permute-start(bf16[1,1,512,128]{3,2,0,1:T(8,128)(2,1)S(1)} %get-tuple-element.226), channel_id=1, source_target_pairs={{0,28},{4,0},{8,4},{12,8},{16,12},{20,16},{24,20},{28,24},{1,29},{... | collective-permute-start | bytes 393224 | tf_op jit(solution)/shard_map/ppermute | solution.py:74
  88.9 26.7 %copy-start.3 = (f32[64,64]{1,0:T(8,128)S(1)}, f32[64,64]{1,0:T(8,128)}, u32[]{:S(2)}) copy-start(f32[64,64]{1,0:T(8,128)} %param.21) | copy-start | bytes 49156
  116.6 8.0 %copy-start.1 = (bf16[1,192,8192]{2,1,0:T(8,128)(2,1)S(1)}, bf16[1,192,8192]{2,1,0:T(8,128)(2,1)}, u32[]{:S(2)}) copy-start(bf16[1,192,8192]{2,1,0:T(8,128)(2,1)} %param.23) | copy-start | bytes 9437188
  126.5 8.9 %collective-permute-start = (bf16[32,8192]{1,0:T(8,128)(2,1)}, bf16[32,8192]{1,0:T(8,128)(2,1)}, u32[]{:S(2)}, u32[]{:S(2)}) collective-permute-start(bf16[32,8192]{1,0:T(8,128)(2,1)} %copy.51), channel_id=1, source_target_pairs={{0,1},{1,2},{2,3},{3,0},{4,5},{5,6},{6,7},{7,4},{8,9},{9,10},{10,1... | collective-permute-start | bytes 1572872 | tf_op jit(solution)/shard_map/while/body/eval_jaxpr/ppermute | solution.py:24
  137.3 8.9 %collective-permute-start = (bf16[32,8192]{1,0:T(8,128)(2,1)}, bf16[32,8192]{1,0:T(8,128)(2,1)}, u32[]{:S(2)}, u32[]{:S(2)}) collective-permute-start(bf16[32,8192]{1,0:T(8,128)(2,1)} %copy.51), channel_id=1, source_target_pairs={{0,1},{1,2},{2,3},{3,0},{4,5},{5,6},{6,7},{7,4},{8,9},{9,10},{10,1... | collective-permute-start | bytes 1572872 | tf_op jit(solution)/shard_map/while/body/eval_jaxpr/ppermute | solution.py:24
  148.1 8.9 %collective-permute-start = (bf16[32,8192]{1,0:T(8,128)(2,1)}, bf16[32,8192]{1,0:T(8,128)(2,1)}, u32[]{:S(2)}, u32[]{:S(2)}) collective-permute-start(bf16[32,8192]{1,0:T(8,128)(2,1)} %copy.51), channel_id=1, source_target_pairs={{0,1},{1,2},{2,3},{3,0},{4,5},{5,6},{6,7},{7,4},{8,9},{9,10},{10,1... | collective-permute-start | bytes 1572872 | tf_op jit(solution)/shard_map/while/body/eval_jaxpr/ppermute | solution.py:24
